TPU v7x, 32 devices: a whole 2x2x4 slice. The times are simulated.
32 devices in a mesh: blk: 16 (over z, y, x), col: 2 (over core).
Axes of the slice: x: 2, y: 2, z: 4, core: 2. Of those that a mesh axis runs over, the one named last changes fastest.
Arguments:
- trial: bfloat16 [32768, 128], P(('blk', 'col')), may hold values from -6 to 6
- omega: float32 [32768], P(('blk', 'col')), may hold values from 0.5 to 6
- table: bfloat16 [64, 128, 128], replicated, may hold values from -0.0625 to 0.0625
- block_type: int32 [256, 72], P(('blk', 'col')), may hold values from 0 to 63
- cycle_offset: int32 [256, 72], P(('blk', 'col')), may hold values from -4 to 4
- source_block: int32 [256, 72], P(('blk', 'col')), may hold values from 0 to 7
Outputs:
- sigma: bfloat16 [32768, 128], P(('blk', 'col'))
- projected: float32 [128, 128], replicated
- basis: float32 [32768, 128], P(('blk', 'col'))
All inputs are finite; a program needn't handle non-finite values.
Results may differ from a plain program's by a relative error of at most 0.006.
Values may be sent and summed in bfloat16 or wider, within the bound.
A program may use at most 64 MiB of HBM per device.

v0:
```python
import jax
import jax.numpy as jnp
from jax import lax
from jax.sharding import PartitionSpec as P

REACH = 4


def from_behind(value, axis, steps):
    count = lax.axis_size(axis)
    pairs = [(source, (source + steps) % count) for source in range(count)]
    return lax.ppermute(value, axis, pairs)


def on_device(trial, omega, table, block_type, cycle_offset, source_block):
    row_count = trial.shape[0]
    vec_count = trial.shape[1]
    pair_block = table.shape[1]
    blocks = row_count // pair_block
    own_slab = trial.reshape(blocks, pair_block, vec_count)
    slabs = {0: own_slab}
    offsets = [offset for offset in range(0 - REACH, REACH + 1) if offset != 0]
    for offset in offsets:
        slabs[offset] = from_behind(own_slab, "blk", 0 - offset)
    stacked = jnp.stack([slabs[offset] for offset in range(0 - REACH, REACH + 1)])
    stacked = stacked.reshape((2 * REACH + 1) * blocks, pair_block, vec_count)
    tile_index = (cycle_offset + REACH) * blocks + source_block
    energy = omega.reshape(blocks, pair_block)

    def one_block(operands):
        kinds, chosen, energy_row, own_rows = operands
        sources = stacked[chosen]
        coeffs = table[kinds]
        coupled = jnp.einsum("jab,jbk->ak", coeffs, sources, preferred_element_type=jnp.float32)
        return (coupled + energy_row[:, None] * own_rows.astype(jnp.float32)).astype(jnp.bfloat16)

    sigma = lax.map(one_block, (block_type, tile_index, energy, own_slab)).reshape(
        row_count, vec_count
    )
    highest = lax.Precision.HIGHEST
    sigma_full = sigma.astype(jnp.float32)
    trial_full = trial.astype(jnp.float32)
    total = row_count * lax.axis_size("blk") * lax.axis_size("col")
    projected = (
        lax.psum(jnp.dot(trial_full.T, sigma_full, precision=highest), ("blk", "col")) / total
    )
    residual = sigma_full - jnp.dot(trial_full, projected, precision=highest)
    gram = lax.psum(jnp.dot(residual.T, residual, precision=highest), ("blk", "col")) / total
    lower = jnp.linalg.cholesky(gram)
    inverse = jax.scipy.linalg.solve_triangular(
        lower, jnp.eye(vec_count, dtype=jnp.float32), lower=True
    )
    basis = jnp.dot(residual, inverse.T, precision=highest)
    return (sigma, projected, basis)


def solution(mesh):
    placed = (
        P(("blk", "col"), None),
        P(("blk", "col")),
        P(),
        P(("blk", "col"), None),
        P(("blk", "col"), None),
        P(("blk", "col"), None),
    )
    return jax.shard_map(
        on_device,
        mesh=mesh,
        in_specs=placed,
        out_specs=(P(("blk", "col"), None), P(), P(("blk", "col"), None)),
        check_vma=False,
    )
```

profile of v0, /device:TPU:1, one launch (start us, length us, event | category | flops | bytes accessed | tf_op | source)
XLA Modules:
  0.0 412.3 jit_solution(719922442792126760)
XLA Ops:
  13.1 4.7 %collective-permute-start.4 = (bf16[8,128,128]{2,1,0:T(8,128)(2,1)}, bf16[8,128,128]{2,1,0:T(8,128)(2,1)S(1)}, u32[]{:S(2)}, u32[]{:S(2)}) collective-permute-start(bf16[8,128,128]{2,1,0:T(8,128)(2,1)} %bitcast.101), channel_id=1, source_target_pairs={{0,30},{2,0},{4,2},{6,4},{8,6},{10,8},{12,10},{14,12},{16,14},{18,... | collective-permute-start | bytes 786440 | tf_op jit(solution)/shard_map/ppermute | solution.py:12
  19.8 4.2 %collective-permute-done.1 = bf16[8,128,128]{2,1,0:T(8,128)(2,1)S(1)} collective-permute-done((bf16[8,128,128]{2,1,0:T(8,128)(2,1)}, bf16[8,128,128]{2,1,0:T(8,128)(2,1)S(1)}, u32[]{:S(2)}, u32[]{:S(2)}) %collective-permute-start.1) | collective-permute-done | bytes 262176 | tf_op jit(solution)/shard_map/ppermute | solution.py:12
  26.4 4.2 %collective-permute-done.2 = bf16[8,128,128]{2,1,0:T(8,128)(2,1)S(1)} collective-permute-done((bf16[8,128,128]{2,1,0:T(8,128)(2,1)}, bf16[8,128,128]{2,1,0:T(8,128)(2,1)S(1)}, u32[]{:S(2)}, u32[]{:S(2)}) %collective-permute-start.2) | collective-permute-done | bytes 262176 | tf_op jit(solution)/shard_map/ppermute | solution.py:12
  32.1 6.1 %collective-permute-done.3 = bf16[8,128,128]{2,1,0:T(8,128)(2,1)S(1)} collective-permute-done((bf16[8,128,128]{2,1,0:T(8,128)(2,1)}, bf16[8,128,128]{2,1,0:T(8,128)(2,1)S(1)}, u32[]{:S(2)}, u32[]{:S(2)}) %collective-permute-start.3) | collective-permute-done | bytes 262176 | tf_op jit(solution)/shard_map/ppermute | solution.py:12
  41.9 84.5 %while.10 = (s32[]{:T(128)}, bf16[8,128,128]{2,1,0:T(8,128)(2,1)S(1)}, s32[8,72]{1,0:T(8,128)}, bf16[64,128,128]{2,1,0:T(8,128)(2,1)}, s32[8,72]{1,0:T(8,128)S(1...) while((s32[]{:T(128)}, ...), condition=%wide.region_1.2_spmd, body=%wide.region_0.1_spmd.sunk | while | flops 302057920 | bytes 14233449 | solution.py:37
  42.6 2.6 gather_fusion
  45.2 4.1 gather_fusion.1
  50.0 2.4 fusion.34
  53.1 2.6 gather_fusion
  55.8 4.1 gather_fusion.1
  60.5 2.4 fusion.34
  63.7 2.6 gather_fusion
  66.3 4.1 gather_fusion.1
  71.1 2.4 fusion.34
  74.3 2.6 gather_fusion
  76.9 4.1 gather_fusion.1
  81.7 2.4 fusion.34
  84.8 2.6 gather_fusion
  87.5 4.1 gather_fusion.1
  92.2 2.4 fusion.34
  95.4 2.6 gather_fusion
  98.0 4.1 gather_fusion.1
  102.8 2.4 fusion.34
  106.0 2.6 gather_fusion
  108.6 4.1 gather_fusion.1
  113.4 2.4 fusion.34
  116.6 2.6 gather_fusion
  119.2 4.1 gather_fusion.1
  127.5 126.7 %all-reduce.3.cloned.1.call-done = f32[128,128]{0,1:T(8,128)} async-done(((f32[128,128]{0,1:T(8,128)}), f32[128,128]{0,1:T(8,128)}) %all-reduce.3.cloned.1.call-update) | async-done | bytes 65552 | tf_op jit(solution)/shard_map/psum | solution.py:45
  258.3 120.5 %all-reduce.5.cloned.1.call-done = f32[128,128]{0,1:T(8,128)} async-done(((f32[128,128]{0,1:T(8,128)}), f32[128,128]{0,1:T(8,128)}) %all-reduce.5.cloned.1.call-update) | async-done | bytes 65552 | tf_op jit(solution)/shard_map/psum | solution.py:48
  380.6 11.7 %cholesky.17 = f32[128,128]{1,0:T(8,128)S(1)} custom-call(f32[128,128]{1,0:T(8,128)S(1)} %fusion.13), custom_call_target="Cholesky" | custom-call | tf_op jit(solution)/shard_map/jit(cholesky)/cholesky | solution.py:49
  393.6 9.8 %custom-call.7 = f32[1,128,128]{1,2,0:T(8,128)S(1)} custom-call(f32[1,128,128]{2,1,0:T(8,128)S(1)} %fusion.10), custom_call_target="InvertDiagBlocksLowerTriangular" | custom-call | tf_op jit(solution)/shard_map/jit(_solve_triangular)/triangular_solve | solution.py:50
  (80 shorter events, 39.3 us)
Async XLA Ops:
  7.2 247.1 %all-reduce.3.cloned.1.call-start = ((), (), s32[]{:S(2)}) async-start(), calls=%async_computation | async-start | bytes 131072 | tf_op jit(solution)/shard_map/psum | solution.py:45
  7.2 11.4 %collective-permute-start = (bf16[8,128,128]{2,1,0:T(8,128)(2,1)}, bf16[8,128,128]{2,1,0:T(8,128)(2,1)S(1)}, u32[]{:S(2)}, u32[]{:S(2)}) collective-permute-start(bf16[8,128,128]{2,1,0:T(8,128)(2,1)} %bitcast.97), channel_id=1, source_target_pairs={{0,8},{2,10},{4,12},{6,14},{8,16},{10,18},{12,20},{14,22},{16,24},... | collective-permute-start | bytes 786440 | tf_op jit(solution)/shard_map/ppermute | solution.py:12
  9.4 14.6 %collective-permute-start.1 = (bf16[8,128,128]{2,1,0:T(8,128)(2,1)}, bf16[8,128,128]{2,1,0:T(8,128)(2,1)S(1)}, u32[]{:S(2)}, u32[]{:S(2)}) collective-permute-start(bf16[8,128,128]{2,1,0:T(8,128)(2,1)} %bitcast.98), channel_id=1, source_target_pairs={{0,6},{2,8},{4,10},{6,12},{8,14},{10,16},{12,18},{14,20},{16,22},{... | collective-permute-start | bytes 786440 | tf_op jit(solution)/shard_map/ppermute | solution.py:12
  11.6 19.0 %collective-permute-start.2 = (bf16[8,128,128]{2,1,0:T(8,128)(2,1)}, bf16[8,128,128]{2,1,0:T(8,128)(2,1)S(1)}, u32[]{:S(2)}, u32[]{:S(2)}) collective-permute-start(bf16[8,128,128]{2,1,0:T(8,128)(2,1)} %bitcast.99), channel_id=1, source_target_pairs={{0,4},{2,6},{4,8},{6,10},{8,12},{10,14},{12,16},{14,18},{16,20},{1... | collective-permute-start | bytes 786440 | tf_op jit(solution)/shard_map/ppermute | solution.py:12
  12.8 25.4 %collective-permute-start.3 = (bf16[8,128,128]{2,1,0:T(8,128)(2,1)}, bf16[8,128,128]{2,1,0:T(8,128)(2,1)S(1)}, u32[]{:S(2)}, u32[]{:S(2)}) collective-permute-start(bf16[8,128,128]{2,1,0:T(8,128)(2,1)} %bitcast.100), channel_id=1, source_target_pairs={{0,2},{2,4},{4,6},{6,8},{8,10},{10,12},{12,14},{14,16},{16,18},{18... | collective-permute-start | bytes 786440 | tf_op jit(solution)/shard_map/ppermute | solution.py:12
  13.1 26.1 %collective-permute-start.4 = (bf16[8,128,128]{2,1,0:T(8,128)(2,1)}, bf16[8,128,128]{2,1,0:T(8,128)(2,1)S(1)}, u32[]{:S(2)}, u32[]{:S(2)}) collective-permute-start(bf16[8,128,128]{2,1,0:T(8,128)(2,1)} %bitcast.101), channel_id=1, source_target_pairs={{0,30},{2,0},{4,2},{6,4},{8,6},{10,8},{12,10},{14,12},{16,14},{18,... | collective-permute-start | bytes 786440 | tf_op jit(solution)/shard_map/ppermute | solution.py:12
  18.6 23.3 %copy-start.1 = (bf16[1024,128]{1,0:T(8,128)(2,1)S(1)}, bf16[1024,128]{1,0:T(8,128)(2,1)}, u32[]{:S(2)}) copy-start(bf16[1024,128]{1,0:T(8,128)(2,1)} %param.8) | copy-start | bytes 786436
  18.6 20.7 %collective-permute-start.5 = (bf16[8,128,128]{2,1,0:T(8,128)(2,1)}, bf16[8,128,128]{2,1,0:T(8,128)(2,1)S(1)}, u32[]{:S(2)}, u32[]{:S(2)}) collective-permute-start(bf16[8,128,128]{2,1,0:T(8,128)(2,1)} %bitcast.102), channel_id=1, source_target_pairs={{0,28},{2,30},{4,0},{6,2},{8,4},{10,6},{12,8},{14,10},{16,12},{18,... | collective-permute-start | bytes 786440 | tf_op jit(solution)/shard_map/ppermute | solution.py:12
  24.0 16.4 %collective-permute-start.6 = (bf16[8,128,128]{2,1,0:T(8,128)(2,1)}, bf16[8,128,128]{2,1,0:T(8,128)(2,1)S(1)}, u32[]{:S(2)}, u32[]{:S(2)}) collective-permute-start(bf16[8,128,128]{2,1,0:T(8,128)(2,1)} %bitcast.103), channel_id=1, source_target_pairs={{0,26},{2,28},{4,30},{6,0},{8,2},{10,4},{12,6},{14,8},{16,10},{18,... | collective-permute-start | bytes 786440 | tf_op jit(solution)/shard_map/ppermute | solution.py:12
  30.5 9.9 %collective-permute-start.7 = (bf16[8,128,128]{2,1,0:T(8,128)(2,1)}, bf16[8,128,128]{2,1,0:T(8,128)(2,1)S(1)}, u32[]{:S(2)}, u32[]{:S(2)}) collective-permute-start(bf16[8,128,128]{2,1,0:T(8,128)(2,1)} %bitcast.104), channel_id=1, source_target_pairs={{0,24},{2,26},{4,28},{6,30},{8,0},{10,2},{12,4},{14,6},{16,8},{18,... | collective-permute-start | bytes 786440 | tf_op jit(solution)/shard_map/ppermute | solution.py:12
  40.5 1.4 copy-start
  126.4 279.1 %copy-start.2 = (bf16[8,128,128]{2,1,0:T(8,128)(2,1)}, bf16[8,128,128]{2,1,0:T(8,128)(2,1)S(1)}, u32[]{:S(2)}) copy-start(bf16[8,128,128]{2,1,0:T(8,128)(2,1)S(1)} %get-tuple-element.45) | copy-start | bytes 786436
  127.3 251.4 %all-reduce.5.cloned.1.call-start = ((), (), s32[]{:S(2)}) async-start(), calls=%async_computation.1 | async-start | bytes 131072 | tf_op jit(solution)/shard_map/psum | solution.py:48
Sparse Core Ops, SparseCore 0:
  127.5 126.7 all-reduce.2
  260.4 118.3 all-reduce.4
where the time goes:
time: 414 us; the launch traced here: 412 us
  waiting for transfers between devices  263 us (64%)
  local copies, waits for them, and re-layouts  62.7 us (15%)
  other arithmetic  31.8 us (8%)
  matrix products  24.9 us (6%)
  starting transfers between devices  15.7 us (4%)
  between operations  14.2 us (3%)
    psum x1, waiting for transfers between devices, on_device(): lax.psum(jnp.dot(trial_full.T, sigma_full, precision=highest), ('blk', 'c...  127 us
    psum x1, waiting for transfers between devices, on_device(): lax.psum(jnp.dot(residual.T, residual, precision=highest), ('blk', 'col'))  120 us
    gather x8, local copies, waits for them, and re-layouts, one_block(): sources = stacked[chosen]  32.8 us
    gather x8, local copies, waits for them, and re-layouts, one_block(): coeffs = table[kinds]  20.7 us
    dot_general x8, matrix products, one_block(): jnp.einsum('jab,jbk->ak', coeffs, sources, preferred_element_type=jnp.flo...  19.6 us
    ppermute x8, starting transfers between devices, from_behind(): return lax.ppermute(value, axis, pairs)  15.7 us
    ppermute x8, waiting for transfers between devices, from_behind(): return lax.ppermute(value, axis, pairs)  15.6 us
    another operation x3, other arithmetic, on_device(): lower = jnp.linalg.cholesky(gram)  12.4 us
  transfers between devices with their start and end apart: 10, of which 6 were waited for; matrix products, arithmetic and copies ran while one was open for 1% of the time, Pallas kernels for 0%

commit v1 on v0

--- a/solution.py
+++ b/solution.py
@@ -45,7 +45,12 @@
         lax.psum(jnp.dot(trial_full.T, sigma_full, precision=highest), ("blk", "col")) / total
     )
     residual = sigma_full - jnp.dot(trial_full, projected, precision=highest)
-    gram = lax.psum(jnp.dot(residual.T, residual, precision=highest), ("blk", "col")) / total
+    gram = (
+        jnp.sum(
+            lax.all_gather(jnp.dot(residual.T, residual, precision=highest), ("blk", "col")), axis=0
+        )
+        / total
+    )
     lower = jnp.linalg.cholesky(gram)
     inverse = jax.scipy.linalg.solve_triangular(
         lower, jnp.eye(vec_count, dtype=jnp.float32), lower=True

time: 414 us -> 349 us (0.84)
  waiting for transfers between devices: 263 us -> 198 us
    psum x1 -> x0, waiting for transfers between devices: 120 us -> none  [on_device(): lax.psum(jnp.dot(residual.T, residual, precision=highest), ('blk', 'col'))]
    all_gather x0 -> x1, waiting for transfers between devices: none -> 55.3 us  [on_device(): lax.all_gather(jnp.dot(residual.T, residual, precision=highest), ('blk',...]
where the time goes in v1:
time: 349 us; the launch traced here: 347 us
  waiting for transfers between devices  198 us (57%)
  local copies, waits for them, and re-layouts  62.7 us (18%)
  other arithmetic  31.8 us (9%)
  matrix products  24.9 us (7%)
  starting transfers between devices  15.7 us (4%)
  between operations  14.2 us (4%)
    psum x1, waiting for transfers between devices, on_device(): lax.psum(jnp.dot(trial_full.T, sigma_full, precision=highest), ('blk', 'c...  127 us
    all_gather x1, waiting for transfers between devices, on_device(): lax.all_gather(jnp.dot(residual.T, residual, precision=highest), ('blk',...  55.3 us
    gather x8, local copies, waits for them, and re-layouts, one_block(): sources = stacked[chosen]  32.8 us
    gather x8, local copies, waits for them, and re-layouts, one_block(): coeffs = table[kinds]  20.7 us
    dot_general x8, matrix products, one_block(): jnp.einsum('jab,jbk->ak', coeffs, sources, preferred_element_type=jnp.flo...  19.6 us
    ppermute x8, starting transfers between devices, from_behind(): return lax.ppermute(value, axis, pairs)  15.7 us
    ppermute x8, waiting for transfers between devices, from_behind(): return lax.ppermute(value, axis, pairs)  15.6 us
    another operation x3, other arithmetic, on_device(): lower = jnp.linalg.cholesky(gram)  12.4 us
  transfers between devices with their start and end apart: 10, of which 6 were waited for; matrix products, arithmetic and copies ran while one was open for 1% of the time, Pallas kernels for 0%

profile of v1, /device:TPU:1, one launch (start us, length us, event | category | flops | bytes accessed | tf_op | source)
XLA Modules:
  0.0 347.1 jit_solution(7446727771374794062)
XLA Ops:
  13.1 4.7 %collective-permute-start.4 = (bf16[8,128,128]{2,1,0:T(8,128)(2,1)}, bf16[8,128,128]{2,1,0:T(8,128)(2,1)S(1)}, u32[]{:S(2)}, u32[]{:S(2)}) collective-permute-start(bf16[8,128,128]{2,1,0:T(8,128)(2,1)} %bitcast.102), channel_id=1, source_target_pairs={{0,30},{2,0},{4,2},{6,4},{8,6},{10,8},{12,10},{14,12},{16,14},{18,... | collective-permute-start | bytes 786440 | tf_op jit(solution)/shard_map/ppermute | solution.py:12
  19.8 4.2 %collective-permute-done.1 = bf16[8,128,128]{2,1,0:T(8,128)(2,1)S(1)} collective-permute-done((bf16[8,128,128]{2,1,0:T(8,128)(2,1)}, bf16[8,128,128]{2,1,0:T(8,128)(2,1)S(1)}, u32[]{:S(2)}, u32[]{:S(2)}) %collective-permute-start.1) | collective-permute-done | bytes 262176 | tf_op jit(solution)/shard_map/ppermute | solution.py:12
  26.4 4.2 %collective-permute-done.2 = bf16[8,128,128]{2,1,0:T(8,128)(2,1)S(1)} collective-permute-done((bf16[8,128,128]{2,1,0:T(8,128)(2,1)}, bf16[8,128,128]{2,1,0:T(8,128)(2,1)S(1)}, u32[]{:S(2)}, u32[]{:S(2)}) %collective-permute-start.2) | collective-permute-done | bytes 262176 | tf_op jit(solution)/shard_map/ppermute | solution.py:12
  32.1 6.1 %collective-permute-done.3 = bf16[8,128,128]{2,1,0:T(8,128)(2,1)S(1)} collective-permute-done((bf16[8,128,128]{2,1,0:T(8,128)(2,1)}, bf16[8,128,128]{2,1,0:T(8,128)(2,1)S(1)}, u32[]{:S(2)}, u32[]{:S(2)}) %collective-permute-start.3) | collective-permute-done | bytes 262176 | tf_op jit(solution)/shard_map/ppermute | solution.py:12
  41.9 84.5 %while.10 = (s32[]{:T(128)}, bf16[8,128,128]{2,1,0:T(8,128)(2,1)S(1)}, s32[8,72]{1,0:T(8,128)}, bf16[64,128,128]{2,1,0:T(8,128)(2,1)}, s32[8,72]{1,0:T(8,128)S(1...) while((s32[]{:T(128)}, ...), condition=%wide.region_1.2_spmd, body=%wide.region_0.1_spmd.sunk | while | flops 302057920 | bytes 14233449 | solution.py:37
  42.6 2.6 gather_fusion
  45.2 4.1 %gather_fusion.1 = bf16[72,128,128]{2,1,0:T(8,128)(2,1)} fusion(bf16[72,128,128]{2,1,0:T(8,128)(2,1)} %get-tuple-element.146, s32[1024]{0:T(1024)S(1)} %pad_clamp_fusion.5), kind=kCustom, calls=%fused_computation.1.clone.1 | custom fusion | bytes 4718880 | tf_op jit(solution)/shard_map/while/body/eval_jaxpr/gather | solution.py:32
  50.0 2.4 fusion.34
  53.1 2.6 gather_fusion
  55.8 4.1 %gather_fusion.1 = bf16[72,128,128]{2,1,0:T(8,128)(2,1)} fusion(bf16[72,128,128]{2,1,0:T(8,128)(2,1)} %get-tuple-element.146, s32[1024]{0:T(1024)S(1)} %pad_clamp_fusion.5), kind=kCustom, calls=%fused_computation.1.clone.1 | custom fusion | bytes 4718880 | tf_op jit(solution)/shard_map/while/body/eval_jaxpr/gather | solution.py:32
  60.5 2.4 fusion.34
  63.7 2.6 gather_fusion
  66.3 4.1 %gather_fusion.1 = bf16[72,128,128]{2,1,0:T(8,128)(2,1)} fusion(bf16[72,128,128]{2,1,0:T(8,128)(2,1)} %get-tuple-element.146, s32[1024]{0:T(1024)S(1)} %pad_clamp_fusion.5), kind=kCustom, calls=%fused_computation.1.clone.1 | custom fusion | bytes 4718880 | tf_op jit(solution)/shard_map/while/body/eval_jaxpr/gather | solution.py:32
  71.1 2.4 fusion.34
  74.3 2.6 gather_fusion
  76.9 4.1 %gather_fusion.1 = bf16[72,128,128]{2,1,0:T(8,128)(2,1)} fusion(bf16[72,128,128]{2,1,0:T(8,128)(2,1)} %get-tuple-element.146, s32[1024]{0:T(1024)S(1)} %pad_clamp_fusion.5), kind=kCustom, calls=%fused_computation.1.clone.1 | custom fusion | bytes 4718880 | tf_op jit(solution)/shard_map/while/body/eval_jaxpr/gather | solution.py:32
  81.7 2.4 fusion.34
  84.8 2.6 gather_fusion
  87.5 4.1 %gather_fusion.1 = bf16[72,128,128]{2,1,0:T(8,128)(2,1)} fusion(bf16[72,128,128]{2,1,0:T(8,128)(2,1)} %get-tuple-element.146, s32[1024]{0:T(1024)S(1)} %pad_clamp_fusion.5), kind=kCustom, calls=%fused_computation.1.clone.1 | custom fusion | bytes 4718880 | tf_op jit(solution)/shard_map/while/body/eval_jaxpr/gather | solution.py:32
  92.2 2.4 fusion.34
  95.4 2.6 gather_fusion
  98.0 4.1 %gather_fusion.1 = bf16[72,128,128]{2,1,0:T(8,128)(2,1)} fusion(bf16[72,128,128]{2,1,0:T(8,128)(2,1)} %get-tuple-element.146, s32[1024]{0:T(1024)S(1)} %pad_clamp_fusion.5), kind=kCustom, calls=%fused_computation.1.clone.1 | custom fusion | bytes 4718880 | tf_op jit(solution)/shard_map/while/body/eval_jaxpr/gather | solution.py:32
  102.8 2.4 fusion.34
  106.0 2.6 gather_fusion
  108.6 4.1 %gather_fusion.1 = bf16[72,128,128]{2,1,0:T(8,128)(2,1)} fusion(bf16[72,128,128]{2,1,0:T(8,128)(2,1)} %get-tuple-element.146, s32[1024]{0:T(1024)S(1)} %pad_clamp_fusion.5), kind=kCustom, calls=%fused_computation.1.clone.1 | custom fusion | bytes 4718880 | tf_op jit(solution)/shard_map/while/body/eval_jaxpr/gather | solution.py:32
  113.4 2.4 fusion.34
  116.6 2.6 gather_fusion
  119.2 4.1 %gather_fusion.1 = bf16[72,128,128]{2,1,0:T(8,128)(2,1)} fusion(bf16[72,128,128]{2,1,0:T(8,128)(2,1)} %get-tuple-element.146, s32[1024]{0:T(1024)S(1)} %pad_clamp_fusion.5), kind=kCustom, calls=%fused_computation.1.clone.1 | custom fusion | bytes 4718880 | tf_op jit(solution)/shard_map/while/body/eval_jaxpr/gather | solution.py:32
  127.5 126.7 %all-reduce.2.cloned.1.call-done = f32[128,128]{0,1:T(8,128)} async-done(((f32[128,128]{0,1:T(8,128)}), f32[128,128]{0,1:T(8,128)}) %all-reduce.2.cloned.1.call-update) | async-done | bytes 65552 | tf_op jit(solution)/shard_map/psum | solution.py:45
  258.3 55.3 %all-gather.3.cloned.1.call-done = f32[4096,128]{1,0:T(8,128)} async-done(((f32[128,128]{1,0:T(8,128)}), f32[4096,128]{1,0:T(8,128)}) %all-gather.3.cloned.1.call-update) | async-done | bytes 2097168 | tf_op jit(solution)/shard_map/all_gather | solution.py:50
  315.4 11.7 %cholesky.17 = f32[128,128]{1,0:T(8,128)S(1)} custom-call(f32[128,128]{1,0:T(8,128)S(1)} %fusion.13), custom_call_target="Cholesky" | custom-call | tf_op jit(solution)/shard_map/jit(cholesky)/cholesky | solution.py:54
  328.4 9.8 %custom-call.7 = f32[1,128,128]{1,2,0:T(8,128)S(1)} custom-call(f32[1,128,128]{2,1,0:T(8,128)S(1)} %fusion.10), custom_call_target="InvertDiagBlocksLowerTriangular" | custom-call | tf_op jit(solution)/shard_map/jit(_solve_triangular)/triangular_solve | solution.py:55
  (80 shorter events, 39.3 us)
Async XLA Ops:
  7.2 247.1 %all-reduce.2.cloned.1.call-start = ((), (), s32[]{:S(2)}) async-start(), calls=%async_computation | async-start | bytes 131072 | tf_op jit(solution)/shard_map/psum | solution.py:45
  7.2 11.4 %collective-permute-start = (bf16[8,128,128]{2,1,0:T(8,128)(2,1)}, bf16[8,128,128]{2,1,0:T(8,128)(2,1)S(1)}, u32[]{:S(2)}, u32[]{:S(2)}) collective-permute-start(bf16[8,128,128]{2,1,0:T(8,128)(2,1)} %bitcast.98), channel_id=1, source_target_pairs={{0,8},{2,10},{4,12},{6,14},{8,16},{10,18},{12,20},{14,22},{16,24},... | collective-permute-start | bytes 786440 | tf_op jit(solution)/shard_map/ppermute | solution.py:12
  9.4 14.6 %collective-permute-start.1 = (bf16[8,128,128]{2,1,0:T(8,128)(2,1)}, bf16[8,128,128]{2,1,0:T(8,128)(2,1)S(1)}, u32[]{:S(2)}, u32[]{:S(2)}) collective-permute-start(bf16[8,128,128]{2,1,0:T(8,128)(2,1)} %bitcast.99), channel_id=1, source_target_pairs={{0,6},{2,8},{4,10},{6,12},{8,14},{10,16},{12,18},{14,20},{16,22},{... | collective-permute-start | bytes 786440 | tf_op jit(solution)/shard_map/ppermute | solution.py:12
  11.6 19.0 %collective-permute-start.2 = (bf16[8,128,128]{2,1,0:T(8,128)(2,1)}, bf16[8,128,128]{2,1,0:T(8,128)(2,1)S(1)}, u32[]{:S(2)}, u32[]{:S(2)}) collective-permute-start(bf16[8,128,128]{2,1,0:T(8,128)(2,1)} %bitcast.100), channel_id=1, source_target_pairs={{0,4},{2,6},{4,8},{6,10},{8,12},{10,14},{12,16},{14,18},{16,20},{1... | collective-permute-start | bytes 786440 | tf_op jit(solution)/shard_map/ppermute | solution.py:12
  12.8 25.4 %collective-permute-start.3 = (bf16[8,128,128]{2,1,0:T(8,128)(2,1)}, bf16[8,128,128]{2,1,0:T(8,128)(2,1)S(1)}, u32[]{:S(2)}, u32[]{:S(2)}) collective-permute-start(bf16[8,128,128]{2,1,0:T(8,128)(2,1)} %bitcast.101), channel_id=1, source_target_pairs={{0,2},{2,4},{4,6},{6,8},{8,10},{10,12},{12,14},{14,16},{16,18},{18... | collective-permute-start | bytes 786440 | tf_op jit(solution)/shard_map/ppermute | solution.py:12
  13.1 26.1 %collective-permute-start.4 = (bf16[8,128,128]{2,1,0:T(8,128)(2,1)}, bf16[8,128,128]{2,1,0:T(8,128)(2,1)S(1)}, u32[]{:S(2)}, u32[]{:S(2)}) collective-permute-start(bf16[8,128,128]{2,1,0:T(8,128)(2,1)} %bitcast.102), channel_id=1, source_target_pairs={{0,30},{2,0},{4,2},{6,4},{8,6},{10,8},{12,10},{14,12},{16,14},{18,... | collective-permute-start | bytes 786440 | tf_op jit(solution)/shard_map/ppermute | solution.py:12
  18.6 23.3 %copy-start.1 = (bf16[1024,128]{1,0:T(8,128)(2,1)S(1)}, bf16[1024,128]{1,0:T(8,128)(2,1)}, u32[]{:S(2)}) copy-start(bf16[1024,128]{1,0:T(8,128)(2,1)} %param.8) | copy-start | bytes 786436
  18.6 20.7 %collective-permute-start.5 = (bf16[8,128,128]{2,1,0:T(8,128)(2,1)}, bf16[8,128,128]{2,1,0:T(8,128)(2,1)S(1)}, u32[]{:S(2)}, u32[]{:S(2)}) collective-permute-start(bf16[8,128,128]{2,1,0:T(8,128)(2,1)} %bitcast.103), channel_id=1, source_target_pairs={{0,28},{2,30},{4,0},{6,2},{8,4},{10,6},{12,8},{14,10},{16,12},{18,... | collective-permute-start | bytes 786440 | tf_op jit(solution)/shard_map/ppermute | solution.py:12
  24.0 16.4 %collective-permute-start.6 = (bf16[8,128,128]{2,1,0:T(8,128)(2,1)}, bf16[8,128,128]{2,1,0:T(8,128)(2,1)S(1)}, u32[]{:S(2)}, u32[]{:S(2)}) collective-permute-start(bf16[8,128,128]{2,1,0:T(8,128)(2,1)} %bitcast.104), channel_id=1, source_target_pairs={{0,26},{2,28},{4,30},{6,0},{8,2},{10,4},{12,6},{14,8},{16,10},{18,... | collective-permute-start | bytes 786440 | tf_op jit(solution)/shard_map/ppermute | solution.py:12
  30.5 9.9 %collective-permute-start.7 = (bf16[8,128,128]{2,1,0:T(8,128)(2,1)}, bf16[8,128,128]{2,1,0:T(8,128)(2,1)S(1)}, u32[]{:S(2)}, u32[]{:S(2)}) collective-permute-start(bf16[8,128,128]{2,1,0:T(8,128)(2,1)} %bitcast.105), channel_id=1, source_target_pairs={{0,24},{2,26},{4,28},{6,30},{8,0},{10,2},{12,4},{14,6},{16,8},{18,... | collective-permute-start | bytes 786440 | tf_op jit(solution)/shard_map/ppermute | solution.py:12
  40.5 1.4 copy-start
  126.4 188.8 %copy-start.2 = (bf16[8,128,128]{2,1,0:T(8,128)(2,1)}, bf16[8,128,128]{2,1,0:T(8,128)(2,1)S(1)}, u32[]{:S(2)}) copy-start(bf16[8,128,128]{2,1,0:T(8,128)(2,1)S(1)} %get-tuple-element.45) | copy-start | bytes 786436
  127.3 186.2 %all-gather.3.cloned.1.call-start = ((), (), s32[]{:S(2)}) async-start(), calls=%async_computation.1 | async-start | bytes 2162688 | tf_op jit(solution)/shard_map/all_gather | solution.py:50
Sparse Core Ops, SparseCore 0:
  127.5 126.7 all-reduce.1
  257.7 55.8 all-gather.2
